TPU v7x, 32 devices: a whole 2x2x4 slice. The times are simulated.
32 devices in a mesh: tok: 8 (over z, core), rep: 4 (over y, x).
Axes of the slice: x: 2, y: 2, z: 4, core: 2. Of those that a mesh axis runs over, the one named last changes fastest.
Arguments:
- hidden_in: bfloat16 [4096, 4096], P('tok', 'rep'), may hold values from -9 to 9
- w_query: bfloat16 [4096, 4096], P(None, 'rep'), may hold values from -2 to 2
- w_key: bfloat16 [4096, 4096], P(None, 'rep'), may hold values from -2 to 2
- w_value: bfloat16 [4096, 4096], P(None, 'rep'), may hold values from -0.09375 to 0.09375
- w_out: bfloat16 [4096, 4096], P('rep'), may hold values from -3 to 3
- q_gain: float32 [4096], P('rep'), may hold values from 0.5 to 6
- k_gain: float32 [4096], P('rep'), may hold values from 0.5 to 6
- post_gain: float32 [4096], P('rep'), may hold values from 0.1 to 1.9
- prompt_lengths: int32 [8], replicated, may hold values from 1 to 2048, as said below
- segment_ids: int32 [4096], replicated, may hold values from 0 to 7, as said below
- deal: int32 [4096], replicated, may hold values from 0 to 4095, as said below
- inverse: int32 [4096], replicated, may hold values from 0 to 4095, as said below
- slots: int32 [4096], replicated, may hold values from 0 to 4095, as said below
Outputs:
- output: bfloat16 [4096, 4096], P('tok', 'rep')
- cache_keys: bfloat16 [4096, 4096], P('tok', 'rep')
- cache_values: bfloat16 [4096, 4096], P('tok', 'rep')
Inputs may be any that keep to these rules, and one draw needn't show every extreme that they name: `prompt_lengths`: the lengths sum to 4096; the longest prompt has exactly 2048 tokens. `segment_ids`: prompts lie in order: prompt s holds the prompt_lengths[s] packed tokens after those of prompts 0 to s - 1. `deal`: A permutation. For any two indices a and b of tok, exactly 64 of the packed tokens a * 512 to (a + 1) * 512 - 1 sit in dealt rows b * 512 to (b + 1) * 512 - 1. inverse[deal[q]] = q for every dealt row q. `slots`: A permutation. For any two indices a and b of tok, exactly 64 of the dealt rows a * 512 to (a + 1) * 512 - 1 have cache rows b * 512 to (b + 1) * 512 - 1.
All inputs are finite; a program needn't handle non-finite values.
Results may differ from a plain program's by a relative error of at most 0.012.
Values may be sent and summed in bfloat16 or wider, within the bound.
A program may use at most 128 MiB of HBM per device.

v0:
```python
import math
import jax
import jax.numpy as jnp
from jax import lax
from jax.sharding import PartitionSpec as P

HEAD_DIM = 128
EPSILON = 1e-06
ROPE_BASE = 500000.0


def rotate(values, positions):
    half_size = values.shape[-1] // 2
    frequency = ROPE_BASE ** (-jnp.arange(half_size, dtype=jnp.float32) * 2.0 / values.shape[-1])
    angles = positions.astype(jnp.float32)[:, None] * frequency[None, :]
    cosine = jnp.cos(angles)[:, None, :]
    sine_part = jnp.sin(angles)[:, None, :]
    lower_half = values[..., :half_size]
    upper_half = values[..., half_size:]
    return jnp.concatenate(
        [
            lower_half * cosine - upper_half * sine_part,
            upper_half * cosine + lower_half * sine_part,
        ],
        axis=-1,
    )


def bucketed(table_rows, row_order, shards):
    picked = table_rows[row_order]
    return picked.reshape(shards, picked.shape[0] // shards, picked.shape[1])


def placement_order(sources, shard_rows):
    local_ids = jnp.arange(sources.shape[0], dtype=jnp.int32)
    arrival = jnp.argsort(sources * shard_rows + local_ids)
    return jnp.argsort(arrival)


def body(
    hidden_in,
    w_query,
    w_key,
    w_value,
    w_out,
    q_gain,
    k_gain,
    post_gain,
    prompt_lengths,
    segment_ids,
    deal,
    inverse,
    slots,
):
    tok_rows, width_dev = hidden_in.shape
    full_width = w_query.shape[0]
    head_size = HEAD_DIM
    heads_dev = width_dev // head_size
    shards = lax.axis_size("tok")
    first_row = lax.axis_index("tok") * tok_rows
    my_packed = lax.dynamic_slice_in_dim(deal, first_row, tok_rows)
    my_segment = segment_ids[my_packed]
    prompt_ids = jnp.arange(prompt_lengths.shape[0], dtype=jnp.int32)
    prompt_starts = jnp.cumsum(prompt_lengths) - prompt_lengths
    my_start = jnp.sum(
        jnp.where(my_segment[:, None] == prompt_ids[None, :], prompt_starts[None, :], 0), axis=1
    )
    positions = my_packed - my_start
    pieces = lax.all_gather(hidden_in, "rep", axis=1, tiled=True)
    query_rows = jnp.dot(pieces, w_query, preferred_element_type=jnp.float32)
    key_rows = jnp.dot(pieces, w_key, preferred_element_type=jnp.float32)
    value_rows = jnp.dot(pieces, w_value, preferred_element_type=jnp.float32)
    query_sums, key_sums = lax.psum(
        (jnp.sum(query_rows * query_rows, axis=1), jnp.sum(key_rows * key_rows, axis=1)), "rep"
    )
    query_rows = (
        query_rows * lax.rsqrt(query_sums / full_width + EPSILON)[:, None] * q_gain[None, :]
    )
    key_rows = key_rows * lax.rsqrt(key_sums / full_width + EPSILON)[:, None] * k_gain[None, :]
    query_rot = rotate(query_rows.reshape(tok_rows, heads_dev, head_size), positions).astype(
        jnp.bfloat16
    )
    key_rot = (
        rotate(key_rows.reshape(tok_rows, heads_dev, head_size), positions)
        .astype(jnp.bfloat16)
        .reshape(tok_rows, width_dev)
    )
    value_half = value_rows.astype(jnp.bfloat16)
    scale = head_size ** (-0.5)

    def attend(state_now, key_block, value_block, key_packed):
        row_top, totals, weighted = state_now
        block_keys = key_block.reshape(key_block.shape[0], heads_dev, head_size)
        block_values = value_block.reshape(value_block.shape[0], heads_dev, head_size)
        key_segment = segment_ids[key_packed]
        allowed = (key_segment[None, :] == my_segment[:, None]) & (
            key_packed[None, :] <= my_packed[:, None]
        )
        scores = (
            jnp.einsum("qhd,khd->hqk", query_rot, block_keys, preferred_element_type=jnp.float32)
            * scale
        )
        masked = jnp.where(allowed[None], scores, -1e30)
        new_top = jnp.maximum(row_top, jnp.max(masked, axis=2))
        weights = jnp.where(allowed[None], jnp.exp(masked - new_top[:, :, None]), 0.0)
        factor = jnp.exp(row_top - new_top)
        totals = totals * factor + jnp.sum(weights, axis=2)
        weighted = weighted * factor[:, :, None] + jnp.einsum(
            "hqk,khd->hqd",
            weights.astype(jnp.bfloat16),
            block_values,
            preferred_element_type=jnp.float32,
        )
        return (new_top, totals, weighted)

    start_state = (
        jnp.full((heads_dev, tok_rows), -1e30, jnp.float32),
        jnp.zeros((heads_dev, tok_rows), jnp.float32),
        jnp.zeros((heads_dev, tok_rows, head_size), jnp.float32),
    )
    owned_rows = lax.dynamic_slice_in_dim(jnp.argsort(slots), first_row, tok_rows)
    my_slots = lax.dynamic_slice_in_dim(slots, first_row, tok_rows)
    slot_order = jnp.argsort(my_slots)
    sent_keys, sent_values = (
        lax.all_to_all(
            bucketed(key_rot, slot_order, shards), "tok", split_axis=0, concat_axis=0, tiled=True
        ),
        lax.all_to_all(
            bucketed(value_half, slot_order, shards), "tok", split_axis=0, concat_axis=0, tiled=True
        ),
    )
    arrival = placement_order(owned_rows // tok_rows, tok_rows)
    cache_keys = sent_keys.reshape(tok_rows, width_dev)[arrival]
    cache_values = sent_values.reshape(tok_rows, width_dev)[arrival]
    pieces = (
        lax.all_gather(key_rot, "tok", axis=0, tiled=True),
        lax.all_gather(value_half, "tok", axis=0, tiled=True),
    )
    key_all = pieces[0]
    block_size = math.gcd(key_all.shape[0], tok_rows)
    block_count = key_all.shape[0] // block_size

    def advance(state_in, block_set):
        return (attend(state_in, block_set[0], block_set[1], block_set[2]), None)

    state_out, _ = lax.scan(
        advance,
        start_state,
        (
            key_all.reshape(block_count, block_size, width_dev),
            pieces[1].reshape(block_count, block_size, width_dev),
            deal.reshape(block_count, block_size),
        ),
    )
    row_top, totals, weighted = state_out
    attended = (
        (weighted / totals[:, :, None])
        .transpose(1, 0, 2)
        .reshape(tok_rows, width_dev)
        .astype(jnp.bfloat16)
    )
    mixed_rows = (
        lax.psum_scatter(
            lax.dot_general(
                w_out, attended, (((0,), (1,)), ((), ())), preferred_element_type=jnp.float32
            ).astype(jnp.bfloat16),
            "rep",
            scatter_dimension=0,
            tiled=True,
        )
        .astype(jnp.float32)
        .T
    )
    mixed_sums = lax.psum(jnp.sum(mixed_rows * mixed_rows, axis=1), "rep")
    normed_rows = (
        mixed_rows * lax.rsqrt(mixed_sums / full_width + EPSILON)[:, None] * post_gain[None, :]
    )
    result_rows = (hidden_in.astype(jnp.float32) + normed_rows).astype(jnp.bfloat16)
    packed_order = jnp.argsort(my_packed)
    returned = lax.all_to_all(
        bucketed(result_rows, packed_order, shards), "tok", split_axis=0, concat_axis=0, tiled=True
    )
    my_dealt = lax.dynamic_slice_in_dim(inverse, first_row, tok_rows)
    output = returned.reshape(tok_rows, width_dev)[placement_order(my_dealt // tok_rows, tok_rows)]
    return (output, cache_keys, cache_values)


def solution(mesh):
    return jax.shard_map(
        body,
        mesh=mesh,
        in_specs=(
            P("tok", "rep"),
            P(None, "rep"),
            P(None, "rep"),
            P(None, "rep"),
            P("rep", None),
            P("rep"),
            P("rep"),
            P("rep"),
            P(),
            P(),
            P(),
            P(),
            P(),
        ),
        out_specs=(P("tok", "rep"), P("tok", "rep"), P("tok", "rep")),
        check_vma=False,
    )
```

profile of v0, /device:TPU:0, one launch (start us, length us, event | category | flops | bytes accessed | tf_op | source)
XLA Modules:
  0.0 586.3 jit_solution(2845161934136654388)
XLA Ops:
  9.6 3.1 gather_fusion.1
  13.8 51.3 %all-gather.4.cloned.1.call-done = bf16[512,4096]{1,0:T(8,128)(2,1)} async-done(((bf16[512,1024]{1,0:T(8,128)(2,1)}), bf16[512,4096]{1,0:T(8,128)(2,1)}) %all-gather.4.cloned.1.call-update) | async-done | bytes 4194320 | tf_op jit(solution)/shard_map/all_gather | solution.py:69
  65.2 10.6 %multiply_reduce_fusion.1 = (f32[512]{0:T(512)S(1)}, f32[512,1024]{1,0:T(8,128)}) fusion(bf16[512,4096]{1,0:T(8,128)(2,1)} %all-gather.4.cloned.1.call-done, bf16[4096,1024]{1,0:T(8,128)(2,1)} %param.17), kind=kOutput, calls=%fused_computation.47 | convolution fusion | flops 4296015360 | bytes 14682112 | tf_op jit(solution)/shard_map/dot_general | solution.py:71
  75.8 7.0 %multiply_reduce_fusion = (f32[512]{0:T(512)S(1)}, f32[512,1024]{1,0:T(8,128)S(1)}) fusion(bf16[512,4096]{1,0:T(8,128)(2,1)S(1)} %copy-done.8, bf16[4096,1024]{1,0:T(8,128)(2,1)} %param.16), kind=kOutput, calls=%fused_computation.43 | convolution fusion | flops 4296015360 | bytes 14682112 | tf_op jit(solution)/shard_map/dot_general | solution.py:70
  82.8 8.9 %all-reduce = (f32[512]{0:T(512)S(1)}, f32[512]{0:T(512)S(1)}) all-reduce(f32[512]{0:T(512)S(1)} %get-tuple-element.181, f32[512]{0:T(512)S(1)} %get-tuple-element.183), channel_id=1, replica_groups=mesh['tok'=8,'rep'=4] {'rep'}, use_global_device_ids=true, to_apply=%region_1.2 | all-reduce | flops 1024 | bytes 8192 | tf_op jit(solution)/shard_map/psum | solution.py:73
  91.8 1.8 multiply_bitcast_fusion.1
  99.6 10.1 %convolution_convert_fusion.1 = bf16[512,1024]{1,0:T(8,128)(2,1)} fusion(bf16[512,4096]{1,0:T(8,128)(2,1)} %all-gather.4.cloned.1.call-done, bf16[4096,1024]{1,0:T(8,128)(2,1)} %param.18), kind=kOutput, calls=%fused_computation.48 | convolution fusion | flops 4295491584 | bytes 13631488 | tf_op jit(solution)/shard_map/dot_general | solution.py:72
  111.4 70.1 %all-gather.6.cloned.1.call-done = bf16[4096,1024]{1,0:T(8,128)(2,1)} async-done(((bf16[512,1024]{1,0:T(8,128)(2,1)}), bf16[4096,1024]{1,0:T(8,128)(2,1)}) %all-gather.6.cloned.1.call-update) | async-done | bytes 8388624 | tf_op jit(solution)/shard_map/all_gather | solution.py:136
  181.6 82.7 %all-gather.8.cloned.1.call-done = bf16[4096,1024]{1,0:T(8,128)(2,1)} async-done(((bf16[512,1024]{1,0:T(8,128)(2,1)}), bf16[4096,1024]{1,0:T(8,128)(2,1)}) %all-gather.8.cloned.1.call-update) | async-done | bytes 8388624 | tf_op jit(solution)/shard_map/all_gather | solution.py:137
  264.3 202.6 %while.15 = (s32[]{:T(128)}, f32[8,512]{1,0:T(8,128)S(1)}, f32[8,512]{1,0:T(8,128)S(1)}, f32[8,512,128]{2,1,0:T(8,128)}, s32[8,512]{1,0:T(8,128)S(1)}, /*index=5...) while((s32[]{:T(128)}, f32[8,512]{1,0:T(8,128)S(1)}, ...), condition=%wide.region_9.10_spmd.clone, body=%wide.region_6.9_spmd.clone.sunk | while | flops 1103387136 | bytes 42231948 | solution.py:146
  264.3 3.1 gather_fusion
  270.0 6.1 %fusion.52 = (f32[8,512]{1,0:T(8,128)S(1)}, f32[8,512,512]{2,1,0:T(8,128)}) fusion(pred[512,512]{0,1:T(8,128)(4,1)S(1)} %compare_and_fusion.2, bf16[512,8,128]{0,2,1:T(8,128)(2,1)S(1)} %bitcast.85, bf16[512,8,128]{2,0,1:T(8,128)(2,1)} %get-tuple-element.307), kind=kOutput, calls=%fused_computation.10.clone.1 | convolution fusion | flops 543158272 | bytes 10764288 | tf_op jit(solution)/shard_map/while/body/eval_jaxpr/qhd,khd->hqk/dot_general | solution.py:100
  276.2 4.5 fusion.53
  281.2 7.9 %fusion.55 = f32[8,512,128]{2,1,0:T(8,128)} fusion(f32[8,512,128]{2,1,0:T(8,128)} %get-tuple-element.288, bf16[512,8,128]{0,2,1:T(8,128)(2,1)S(1)} %bitcast.89, f32[8,512,512]{2,1,0:T(8,128)} %get-tuple-element.268, f32[8,512]{1,0:T(8,128)S(1)} %select_maximum_fusion.2, pred[512,512]{0,1:T(8,128)(4,1)S(1)} %compare_and_fusion.2, ...), kind=kOutput, calls=%fused_computation.16.clone.1 | convolution fusion | flops 548929536 | bytes 13926401 | tf_op jit(solution)/shard_map/while/body/eval_jaxpr/hqk,khd->hqd/dot_general | solution.py:108
  289.1 3.1 gather_fusion
  294.8 6.1 %fusion.52 = (f32[8,512]{1,0:T(8,128)S(1)}, f32[8,512,512]{2,1,0:T(8,128)}) fusion(pred[512,512]{0,1:T(8,128)(4,1)S(1)} %compare_and_fusion.2, bf16[512,8,128]{0,2,1:T(8,128)(2,1)S(1)} %bitcast.85, bf16[512,8,128]{2,0,1:T(8,128)(2,1)} %get-tuple-element.307), kind=kOutput, calls=%fused_computation.10.clone.1 | convolution fusion | flops 543158272 | bytes 10764288 | tf_op jit(solution)/shard_map/while/body/eval_jaxpr/qhd,khd->hqk/dot_general | solution.py:100
  301.0 4.5 fusion.53
  306.0 8.5 %fusion.55 = f32[8,512,128]{2,1,0:T(8,128)} fusion(f32[8,512,128]{2,1,0:T(8,128)} %get-tuple-element.288, bf16[512,8,128]{0,2,1:T(8,128)(2,1)S(1)} %bitcast.89, f32[8,512,512]{2,1,0:T(8,128)} %get-tuple-element.268, f32[8,512]{1,0:T(8,128)S(1)} %select_maximum_fusion.2, pred[512,512]{0,1:T(8,128)(4,1)S(1)} %compare_and_fusion.2, ...), kind=kOutput, calls=%fused_computation.16.clone.1 | convolution fusion | flops 548929536 | bytes 13926401 | tf_op jit(solution)/shard_map/while/body/eval_jaxpr/hqk,khd->hqd/dot_general | solution.py:108
  314.5 3.1 gather_fusion
  320.2 6.1 %fusion.52 = (f32[8,512]{1,0:T(8,128)S(1)}, f32[8,512,512]{2,1,0:T(8,128)}) fusion(pred[512,512]{0,1:T(8,128)(4,1)S(1)} %compare_and_fusion.2, bf16[512,8,128]{0,2,1:T(8,128)(2,1)S(1)} %bitcast.85, bf16[512,8,128]{2,0,1:T(8,128)(2,1)} %get-tuple-element.307), kind=kOutput, calls=%fused_computation.10.clone.1 | convolution fusion | flops 543158272 | bytes 10764288 | tf_op jit(solution)/shard_map/while/body/eval_jaxpr/qhd,khd->hqk/dot_general | solution.py:100
  326.4 4.5 fusion.53
  331.4 8.5 %fusion.55 = f32[8,512,128]{2,1,0:T(8,128)} fusion(f32[8,512,128]{2,1,0:T(8,128)} %get-tuple-element.288, bf16[512,8,128]{0,2,1:T(8,128)(2,1)S(1)} %bitcast.89, f32[8,512,512]{2,1,0:T(8,128)} %get-tuple-element.268, f32[8,512]{1,0:T(8,128)S(1)} %select_maximum_fusion.2, pred[512,512]{0,1:T(8,128)(4,1)S(1)} %compare_and_fusion.2, ...), kind=kOutput, calls=%fused_computation.16.clone.1 | convolution fusion | flops 548929536 | bytes 13926401 | tf_op jit(solution)/shard_map/while/body/eval_jaxpr/hqk,khd->hqd/dot_general | solution.py:108
  339.9 3.1 gather_fusion
  345.6 6.1 %fusion.52 = (f32[8,512]{1,0:T(8,128)S(1)}, f32[8,512,512]{2,1,0:T(8,128)}) fusion(pred[512,512]{0,1:T(8,128)(4,1)S(1)} %compare_and_fusion.2, bf16[512,8,128]{0,2,1:T(8,128)(2,1)S(1)} %bitcast.85, bf16[512,8,128]{2,0,1:T(8,128)(2,1)} %get-tuple-element.307), kind=kOutput, calls=%fused_computation.10.clone.1 | convolution fusion | flops 543158272 | bytes 10764288 | tf_op jit(solution)/shard_map/while/body/eval_jaxpr/qhd,khd->hqk/dot_general | solution.py:100
  351.8 4.5 fusion.53
  356.8 8.5 %fusion.55 = f32[8,512,128]{2,1,0:T(8,128)} fusion(f32[8,512,128]{2,1,0:T(8,128)} %get-tuple-element.288, bf16[512,8,128]{0,2,1:T(8,128)(2,1)S(1)} %bitcast.89, f32[8,512,512]{2,1,0:T(8,128)} %get-tuple-element.268, f32[8,512]{1,0:T(8,128)S(1)} %select_maximum_fusion.2, pred[512,512]{0,1:T(8,128)(4,1)S(1)} %compare_and_fusion.2, ...), kind=kOutput, calls=%fused_computation.16.clone.1 | convolution fusion | flops 548929536 | bytes 13926401 | tf_op jit(solution)/shard_map/while/body/eval_jaxpr/hqk,khd->hqd/dot_general | solution.py:108
  365.3 3.1 gather_fusion
  371.0 6.1 %fusion.52 = (f32[8,512]{1,0:T(8,128)S(1)}, f32[8,512,512]{2,1,0:T(8,128)}) fusion(pred[512,512]{0,1:T(8,128)(4,1)S(1)} %compare_and_fusion.2, bf16[512,8,128]{0,2,1:T(8,128)(2,1)S(1)} %bitcast.85, bf16[512,8,128]{2,0,1:T(8,128)(2,1)} %get-tuple-element.307), kind=kOutput, calls=%fused_computation.10.clone.1 | convolution fusion | flops 543158272 | bytes 10764288 | tf_op jit(solution)/shard_map/while/body/eval_jaxpr/qhd,khd->hqk/dot_general | solution.py:100
  377.2 4.5 fusion.53
  382.2 8.5 %fusion.55 = f32[8,512,128]{2,1,0:T(8,128)} fusion(f32[8,512,128]{2,1,0:T(8,128)} %get-tuple-element.288, bf16[512,8,128]{0,2,1:T(8,128)(2,1)S(1)} %bitcast.89, f32[8,512,512]{2,1,0:T(8,128)} %get-tuple-element.268, f32[8,512]{1,0:T(8,128)S(1)} %select_maximum_fusion.2, pred[512,512]{0,1:T(8,128)(4,1)S(1)} %compare_and_fusion.2, ...), kind=kOutput, calls=%fused_computation.16.clone.1 | convolution fusion | flops 548929536 | bytes 13926401 | tf_op jit(solution)/shard_map/while/body/eval_jaxpr/hqk,khd->hqd/dot_general | solution.py:108
  390.7 3.1 gather_fusion
  396.4 6.1 %fusion.52 = (f32[8,512]{1,0:T(8,128)S(1)}, f32[8,512,512]{2,1,0:T(8,128)}) fusion(pred[512,512]{0,1:T(8,128)(4,1)S(1)} %compare_and_fusion.2, bf16[512,8,128]{0,2,1:T(8,128)(2,1)S(1)} %bitcast.85, bf16[512,8,128]{2,0,1:T(8,128)(2,1)} %get-tuple-element.307), kind=kOutput, calls=%fused_computation.10.clone.1 | convolution fusion | flops 543158272 | bytes 10764288 | tf_op jit(solution)/shard_map/while/body/eval_jaxpr/qhd,khd->hqk/dot_general | solution.py:100
  402.5 4.5 fusion.53
  407.6 8.5 %fusion.55 = f32[8,512,128]{2,1,0:T(8,128)} fusion(f32[8,512,128]{2,1,0:T(8,128)} %get-tuple-element.288, bf16[512,8,128]{0,2,1:T(8,128)(2,1)S(1)} %bitcast.89, f32[8,512,512]{2,1,0:T(8,128)} %get-tuple-element.268, f32[8,512]{1,0:T(8,128)S(1)} %select_maximum_fusion.2, pred[512,512]{0,1:T(8,128)(4,1)S(1)} %compare_and_fusion.2, ...), kind=kOutput, calls=%fused_computation.16.clone.1 | convolution fusion | flops 548929536 | bytes 13926401 | tf_op jit(solution)/shard_map/while/body/eval_jaxpr/hqk,khd->hqd/dot_general | solution.py:108
  416.1 3.1 gather_fusion
  421.8 6.1 %fusion.52 = (f32[8,512]{1,0:T(8,128)S(1)}, f32[8,512,512]{2,1,0:T(8,128)}) fusion(pred[512,512]{0,1:T(8,128)(4,1)S(1)} %compare_and_fusion.2, bf16[512,8,128]{0,2,1:T(8,128)(2,1)S(1)} %bitcast.85, bf16[512,8,128]{2,0,1:T(8,128)(2,1)} %get-tuple-element.307), kind=kOutput, calls=%fused_computation.10.clone.1 | convolution fusion | flops 543158272 | bytes 10764288 | tf_op jit(solution)/shard_map/while/body/eval_jaxpr/qhd,khd->hqk/dot_general | solution.py:100
  427.9 4.5 fusion.53
  433.0 8.5 %fusion.55 = f32[8,512,128]{2,1,0:T(8,128)} fusion(f32[8,512,128]{2,1,0:T(8,128)} %get-tuple-element.288, bf16[512,8,128]{0,2,1:T(8,128)(2,1)S(1)} %bitcast.89, f32[8,512,512]{2,1,0:T(8,128)} %get-tuple-element.268, f32[8,512]{1,0:T(8,128)S(1)} %select_maximum_fusion.2, pred[512,512]{0,1:T(8,128)(4,1)S(1)} %compare_and_fusion.2, ...), kind=kOutput, calls=%fused_computation.16.clone.1 | convolution fusion | flops 548929536 | bytes 13926401 | tf_op jit(solution)/shard_map/while/body/eval_jaxpr/hqk,khd->hqd/dot_general | solution.py:108
  441.5 3.1 gather_fusion
  447.2 6.1 %fusion.52 = (f32[8,512]{1,0:T(8,128)S(1)}, f32[8,512,512]{2,1,0:T(8,128)}) fusion(pred[512,512]{0,1:T(8,128)(4,1)S(1)} %compare_and_fusion.2, bf16[512,8,128]{0,2,1:T(8,128)(2,1)S(1)} %bitcast.85, bf16[512,8,128]{2,0,1:T(8,128)(2,1)} %get-tuple-element.307), kind=kOutput, calls=%fused_computation.10.clone.1 | convolution fusion | flops 543158272 | bytes 10764288 | tf_op jit(solution)/shard_map/while/body/eval_jaxpr/qhd,khd->hqk/dot_general | solution.py:100
  453.3 4.5 fusion.53
  458.4 8.5 %fusion.55 = f32[8,512,128]{2,1,0:T(8,128)} fusion(f32[8,512,128]{2,1,0:T(8,128)} %get-tuple-element.288, bf16[512,8,128]{0,2,1:T(8,128)(2,1)S(1)} %bitcast.89, f32[8,512,512]{2,1,0:T(8,128)} %get-tuple-element.268, f32[8,512]{1,0:T(8,128)S(1)} %select_maximum_fusion.2, pred[512,512]{0,1:T(8,128)(4,1)S(1)} %compare_and_fusion.2, ...), kind=kOutput, calls=%fused_computation.16.clone.1 | convolution fusion | flops 548929536 | bytes 13926401 | tf_op jit(solution)/shard_map/while/body/eval_jaxpr/hqk,khd->hqd/dot_general | solution.py:108
  466.9 1.9 copy.43
  469.1 9.5 %fusion.13 = bf16[4096,512]{0,1:T(8,128)(2,1)} fusion(bf16[512,1024]{0,1:T(8,128)(2,1)S(1)} %bitcast.95, bf16[1024,4096]{1,0:T(8,128)(2,1)} %param.19), kind=kOutput, calls=%fused_computation.31 | convolution fusion | flops 4297064448 | bytes 13631488 | tf_op jit(solution)/shard_map/dot_general | solution.py:164
  479.4 3.8 sort.107
  483.2 2.8 gather_fusion.4
  485.9 3.9 all-to-all-start.1
  489.9 2.8 gather_fusion.6
  492.6 23.5 %all-to-all-done.1 = bf16[8,64,1024]{2,1,0:T(8,128)(2,1)S(1)} async-done(((bf16[8,64,1024]{2,1,0:T(8,128)(2,1)}), bf16[8,64,1024]{2,1,0:T(8,128)(2,1)S(1)}, u32[]{:S(2)}, u32[]{:S(2)}) %all-to-all-start.1) | async-done | bytes 1048608 | tf_op jit(solution)/shard_map/all_to_all | solution.py:125
  516.1 3.6 all-to-all-start.2
  519.7 3.8 sort.104
  523.5 6.4 %reduce-scatter.2.cloned.1.call-done = bf16[1024,512]{0,1:T(8,128)(2,1)} async-done(((bf16[4096,512]{0,1:T(8,128)(2,1)}), bf16[1024,512]{0,1:T(8,128)(2,1)}) %reduce-scatter.2.cloned.1.call-update) | async-done | bytes 1048592 | tf_op jit(solution)/shard_map/reduce_scatter | solution.py:163
  531.4 8.9 %psum.23 = f32[512]{0:T(512)S(1)} all-reduce(f32[512]{0:T(512)S(1)} %fusion.14), channel_id=1, replica_groups=mesh['tok'=8,'rep'=4] {'rep'}, use_global_device_ids=true, to_apply=%region_12.13 | all-reduce | flops 512 | bytes 4096 | tf_op jit(solution)/shard_map/psum | solution.py:174
  540.3 2.0 fusion.18
  542.3 2.8 gather_fusion.2
  546.2 3.6 all-to-all-start
  549.8 5.8 sort.108
  556.3 3.8 sort.105
  560.1 3.8 sort.106
  563.9 3.8 sort.109
  567.6 3.8 sort.110
  571.4 2.8 gather_fusion.5
  574.2 2.8 gather_fusion.7
  577.0 2.8 gather_fusion.3
  (143 shorter events, 40.5 us)
Async XLA Ops:
  7.2 5.6 copy-start.9
  7.2 2.4 copy-start
  7.2 58.0 %all-gather.4.cloned.1.call-start = ((), (), s32[]{:S(2)}) async-start(), calls=%async_computation.4 | async-start | bytes 5242880 | tf_op jit(solution)/shard_map/all_gather | solution.py:69
  7.9 173.7 %all-gather.6.cloned.1.call-start = ((), (), s32[]{:S(2)}) async-start(), calls=%async_computation.5 | async-start | bytes 9437184 | tf_op jit(solution)/shard_map/all_gather | solution.py:136
  65.2 10.6 %copy-start.8 = (bf16[512,4096]{1,0:T(8,128)(2,1)S(1)}, bf16[512,4096]{1,0:T(8,128)(2,1)}, u32[]{:S(2)}) copy-start(bf16[512,4096]{1,0:T(8,128)(2,1)} %all-gather.4.cloned.1.call-done) | copy-start | bytes 12582916
  75.8 16.0 %copy-start.5 = (f32[1024]{0:T(1024)S(1)}, f32[1024]{0:T(1024)}, u32[]{:S(2)}) copy-start(f32[1024]{0:T(1024)} %param.21) | copy-start | bytes 12292
  94.1 0.7 copy-start.6
  99.4 10.5 %copy-start.3 = (s32[4096]{0:T(1024)S(1)}, s32[4096]{0:T(1024)}, u32[]{:S(2)}) copy-start(s32[4096]{0:T(1024)} %param.25) | copy-start | bytes 49156
  99.4 164.9 %all-gather.8.cloned.1.call-start = ((), (), s32[]{:S(2)}) async-start(), calls=%async_computation.6 | async-start | bytes 9437184 | tf_op jit(solution)/shard_map/all_gather | solution.py:137
  109.8 420.1 %reduce-scatter.2.cloned.1.call-start = ((), (), s32[]{:S(2)}) async-start(), calls=%async_computation.7 | async-start | bytes 5242880 | tf_op jit(solution)/shard_map/reduce_scatter | solution.py:163
  478.6 0.7 copy-start.4
  478.6 4.6 copy-start.1
  485.9 3.9 copy-start.2
  485.9 30.2 %all-to-all-start.1 = ((bf16[8,64,1024]{2,1,0:T(8,128)(2,1)}), bf16[8,64,1024]{2,1,0:T(8,128)(2,1)S(1)}, u32[]{:S(2)}, u32[]{:S(2)}) async-start(bf16[8,64,1024]{2,1,0:T(8,128)(2,1)} %bitcast.10), calls=%async_computation.2 | async-start | bytes 2097152 | tf_op jit(solution)/shard_map/all_to_all | solution.py:125
  492.6 47.7 %copy-start.7 = (f32[1024]{0:T(1024)S(1)}, f32[1024]{0:T(1024)}, u32[]{:S(2)}) copy-start(f32[1024]{0:T(1024)} %param.22) | copy-start | bytes 12292
  516.1 30.1 %all-to-all-start.2 = ((bf16[8,64,1024]{2,1,0:T(8,128)(2,1)}), bf16[8,64,1024]{2,1,0:T(8,128)(2,1)S(1)}, u32[]{:S(2)}, u32[]{:S(2)}) async-start(bf16[8,64,1024]{2,1,0:T(8,128)(2,1)} %bitcast.12), calls=%async_computation.3 | async-start | bytes 2097152 | tf_op jit(solution)/shard_map/all_to_all | solution.py:128
  546.2 30.8 %all-to-all-start = ((bf16[8,64,1024]{2,1,0:T(8,128)(2,1)}), bf16[8,64,1024]{2,1,0:T(8,128)(2,1)S(1)}, u32[]{:S(2)}, u32[]{:S(2)}) async-start(bf16[8,64,1024]{2,1,0:T(8,128)(2,1)} %bitcast.92), calls=%async_computation.1 | async-start | bytes 2097152 | tf_op jit(solution)/shard_map/all_to_all | solution.py:180
Sparse Core Ops, SparseCore 0:
  9.8 55.2 all-gather.3
  99.5 82.0 all-gather.5
  183.8 80.5 all-gather.7
  478.7 51.1 reduce-scatter.1
where the time goes:
time: 587 us; the launch traced here: 586 us
  waiting for transfers between devices  236 us (40%)
  matrix products  153 us (26%)
  other arithmetic  80.8 us (14%)
  local copies, waits for them, and re-layouts  72.4 us (12%)
  blocking collectives  17.9 us (3%)
  between operations  14.1 us (2%)
  starting transfers between devices  11.4 us (2%)
    all_gather x1, waiting for transfers between devices, body(): lax.all_gather(value_half, 'tok', axis=0, tiled=True)  82.7 us
    all_gather x1, waiting for transfers between devices, body(): lax.all_gather(key_rot, 'tok', axis=0, tiled=True)  70.1 us
    dot_general x8, matrix products, attend(): jnp.einsum('hqk,khd->hqd', weights.astype(jnp.bfloat16), block_values, pr...  67.1 us
    all_gather x1, waiting for transfers between devices, body(): pieces = lax.all_gather(hidden_in, 'rep', axis=1, tiled=True)  51.3 us
    dot_general x8, matrix products, attend(): jnp.einsum('qhd,khd->hqk', query_rot, block_keys, preferred_element_type=...  49 us
    reduce_sum x8, other arithmetic, attend(): totals = totals * factor + jnp.sum(weights, axis=2)  35.9 us
    gather x8, local copies, waits for them, and re-layouts, attend(): key_segment = segment_ids[key_packed]  25.1 us
    all_to_all x1, waiting for transfers between devices, body(): lax.all_to_all(bucketed(key_rot, slot_order, shards), 'tok', split_axis=0...  23.5 us
  transfers between devices with their start and end apart: 7, of which 6 were waited for; matrix products, arithmetic and copies ran while one was open for 11% of the time, Pallas kernels for 0%

commit v1 on v0

--- a/solution.py
+++ b/solution.py
@@ -66,7 +66,9 @@
         jnp.where(my_segment[:, None] == prompt_ids[None, :], prompt_starts[None, :], 0), axis=1
     )
     positions = my_packed - my_start
-    pieces = lax.all_gather(hidden_in, "rep", axis=1, tiled=True)
+    pieces = jnp.concatenate(
+        lax.all_to_all(jnp.stack([hidden_in] * lax.axis_size("rep")), "rep", 0, 0), axis=1
+    )
     query_rows = jnp.dot(pieces, w_query, preferred_element_type=jnp.float32)
     key_rows = jnp.dot(pieces, w_key, preferred_element_type=jnp.float32)
     value_rows = jnp.dot(pieces, w_value, preferred_element_type=jnp.float32)

time: 587 us -> 589 us (level)
  waiting for transfers between devices: 236 us -> 229 us
    all_gather x1 -> x0, waiting for transfers between devices: 51.3 us -> none  [body(): pieces = lax.all_gather(hidden_in, 'rep', axis=1, tiled=True)]
    all_to_all x0 -> x1, waiting for transfers between devices: none -> 44 us  [body(): lax.all_to_all(jnp.stack([hidden_in] * lax.axis_size('rep')), 'rep', 0, 0)]
where the time goes in v1:
time: 589 us; the launch traced here: 588 us
  waiting for transfers between devices  229 us (39%)
  matrix products  155 us (26%)
  other arithmetic  79.5 us (13%)
  local copies, waits for them, and re-layouts  76.1 us (13%)
  blocking collectives  18.1 us (3%)
  starting transfers between devices  16.5 us (3%)
  between operations  14 us (2%)
    all_gather x1, waiting for transfers between devices, body(): lax.all_gather(value_half, 'tok', axis=0, tiled=True)  82.7 us
    all_gather x1, waiting for transfers between devices, body(): lax.all_gather(key_rot, 'tok', axis=0, tiled=True)  70.9 us
    dot_general x8, matrix products, attend(): jnp.einsum('hqk,khd->hqd', weights.astype(jnp.bfloat16), block_values, pr...  67.1 us
    dot_general x8, matrix products, attend(): jnp.einsum('qhd,khd->hqk', query_rot, block_keys, preferred_element_type=...  49 us
    all_to_all x1, waiting for transfers between devices, body(): lax.all_to_all(jnp.stack([hidden_in] * lax.axis_size('rep')), 'rep', 0, 0)  44 us
    reduce_sum x8, other arithmetic, attend(): totals = totals * factor + jnp.sum(weights, axis=2)  35.9 us
    gather x8, local copies, waits for them, and re-layouts, attend(): key_segment = segment_ids[key_packed]  25.1 us
    all_to_all x1, waiting for transfers between devices, body(): lax.all_to_all(bucketed(key_rot, slot_order, shards), 'tok', split_axis=0...  23.4 us
  transfers between devices with their start and end apart: 7, of which 6 were waited for; matrix products, arithmetic and copies ran while one was open for 11% of the time, Pallas kernels for 0%

profile of v1, /device:TPU:0, one launch (start us, length us, event | category | flops | bytes accessed | tf_op | source)
XLA Modules:
  0.0 587.9 jit_solution(13691495882081726248)
XLA Ops:
  8.7 2.3 stack.2
  10.9 5.3 all-to-all-start
  16.5 3.1 gather_fusion.1
  20.8 44.0 %all-to-all-done = bf16[4,512,1024]{1,2,0:T(8,128)(2,1)} async-done(((bf16[4,512,1024]{1,2,0:T(8,128)(2,1)}), bf16[4,512,1024]{1,2,0:T(8,128)(2,1)}, u32[]{:S(2)}, u32[]{:S(2)}) %all-to-all-start) | async-done | bytes 4194336 | tf_op jit(solution)/shard_map/all_to_all | solution.py:70
  64.8 10.5 %multiply_reduce_fusion.1 = (f32[512]{0:T(512)S(1)}, f32[512,1024]{1,0:T(8,128)}) fusion(bf16[512,4096]{0,1:T(8,128)(2,1)} %bitcast.1, bf16[4096,1024]{1,0:T(8,128)(2,1)} %param.17), kind=kOutput, calls=%fused_computation.47 | convolution fusion | flops 4296015360 | bytes 14682112 | tf_op jit(solution)/shard_map/dot_general | solution.py:73
  75.4 8.4 %multiply_reduce_fusion = (f32[512]{0:T(512)S(1)}, f32[512,1024]{1,0:T(8,128)S(1)}) fusion(bf16[512,4096]{0,1:T(8,128)(2,1)} %bitcast.1, bf16[4096,1024]{1,0:T(8,128)(2,1)} %param.16), kind=kOutput, calls=%fused_computation.43 | convolution fusion | flops 4296015360 | bytes 14682112 | tf_op jit(solution)/shard_map/dot_general | solution.py:72
  83.7 9.1 %all-reduce = (f32[512]{0:T(512)S(1)}, f32[512]{0:T(512)S(1)}) all-reduce(f32[512]{0:T(512)S(1)} %get-tuple-element.181, f32[512]{0:T(512)S(1)} %get-tuple-element.183), channel_id=1, replica_groups=mesh['tok'=8,'rep'=4] {'rep'}, use_global_device_ids=true, to_apply=%region_1.2 | all-reduce | flops 1024 | bytes 8192 | tf_op jit(solution)/shard_map/psum | solution.py:75
  100.5 10.1 %convolution_convert_fusion.1 = bf16[512,1024]{1,0:T(8,128)(2,1)} fusion(bf16[512,4096]{0,1:T(8,128)(2,1)} %bitcast.1, bf16[4096,1024]{1,0:T(8,128)(2,1)} %param.18), kind=kOutput, calls=%fused_computation.48 | convolution fusion | flops 4295491584 | bytes 13631488 | tf_op jit(solution)/shard_map/dot_general | solution.py:74
  112.3 70.9 %all-gather.3.cloned.1.call-done = bf16[4096,1024]{1,0:T(8,128)(2,1)} async-done(((bf16[512,1024]{1,0:T(8,128)(2,1)}), bf16[4096,1024]{1,0:T(8,128)(2,1)}) %all-gather.3.cloned.1.call-update) | async-done | bytes 8388624 | tf_op jit(solution)/shard_map/all_gather | solution.py:138
  183.2 82.7 %all-gather.5.cloned.1.call-done = bf16[4096,1024]{1,0:T(8,128)(2,1)} async-done(((bf16[512,1024]{1,0:T(8,128)(2,1)}), bf16[4096,1024]{1,0:T(8,128)(2,1)}) %all-gather.5.cloned.1.call-update) | async-done | bytes 8388624 | tf_op jit(solution)/shard_map/all_gather | solution.py:139
  265.9 202.6 %while.15 = (s32[]{:T(128)}, f32[8,512]{1,0:T(8,128)S(1)}, f32[8,512]{1,0:T(8,128)S(1)}, f32[8,512,128]{2,1,0:T(8,128)}, s32[8,512]{1,0:T(8,128)S(1)}, /*index=5...) while((s32[]{:T(128)}, f32[8,512]{1,0:T(8,128)S(1)}, ...), condition=%wide.region_9.10_spmd.clone, body=%wide.region_6.9_spmd.clone.sunk | while | flops 1103387136 | bytes 42231948 | solution.py:148
  266.0 3.1 gather_fusion
  271.7 6.1 %fusion.52 = (f32[8,512]{1,0:T(8,128)S(1)}, f32[8,512,512]{2,1,0:T(8,128)}) fusion(pred[512,512]{0,1:T(8,128)(4,1)S(1)} %compare_and_fusion.2, bf16[512,8,128]{0,2,1:T(8,128)(2,1)S(1)} %bitcast.88, bf16[512,8,128]{2,0,1:T(8,128)(2,1)} %get-tuple-element.307), kind=kOutput, calls=%fused_computation.10.clone.1 | convolution fusion | flops 543158272 | bytes 10764288 | tf_op jit(solution)/shard_map/while/body/eval_jaxpr/qhd,khd->hqk/dot_general | solution.py:102
  277.8 4.5 fusion.53
  282.9 7.9 %fusion.55 = f32[8,512,128]{2,1,0:T(8,128)} fusion(f32[8,512,128]{2,1,0:T(8,128)} %get-tuple-element.288, bf16[512,8,128]{0,2,1:T(8,128)(2,1)S(1)} %bitcast.92, f32[8,512,512]{2,1,0:T(8,128)} %get-tuple-element.268, f32[8,512]{1,0:T(8,128)S(1)} %select_maximum_fusion.2, pred[512,512]{0,1:T(8,128)(4,1)S(1)} %compare_and_fusion.2, ...), kind=kOutput, calls=%fused_computation.16.clone.1 | convolution fusion | flops 548929536 | bytes 13926401 | tf_op jit(solution)/shard_map/while/body/eval_jaxpr/hqk,khd->hqd/dot_general | solution.py:110
  290.8 3.1 gather_fusion
  296.5 6.1 %fusion.52 = (f32[8,512]{1,0:T(8,128)S(1)}, f32[8,512,512]{2,1,0:T(8,128)}) fusion(pred[512,512]{0,1:T(8,128)(4,1)S(1)} %compare_and_fusion.2, bf16[512,8,128]{0,2,1:T(8,128)(2,1)S(1)} %bitcast.88, bf16[512,8,128]{2,0,1:T(8,128)(2,1)} %get-tuple-element.307), kind=kOutput, calls=%fused_computation.10.clone.1 | convolution fusion | flops 543158272 | bytes 10764288 | tf_op jit(solution)/shard_map/while/body/eval_jaxpr/qhd,khd->hqk/dot_general | solution.py:102
  302.6 4.5 fusion.53
  307.7 8.5 %fusion.55 = f32[8,512,128]{2,1,0:T(8,128)} fusion(f32[8,512,128]{2,1,0:T(8,128)} %get-tuple-element.288, bf16[512,8,128]{0,2,1:T(8,128)(2,1)S(1)} %bitcast.92, f32[8,512,512]{2,1,0:T(8,128)} %get-tuple-element.268, f32[8,512]{1,0:T(8,128)S(1)} %select_maximum_fusion.2, pred[512,512]{0,1:T(8,128)(4,1)S(1)} %compare_and_fusion.2, ...), kind=kOutput, calls=%fused_computation.16.clone.1 | convolution fusion | flops 548929536 | bytes 13926401 | tf_op jit(solution)/shard_map/while/body/eval_jaxpr/hqk,khd->hqd/dot_general | solution.py:110
  316.2 3.1 gather_fusion
  321.9 6.1 %fusion.52 = (f32[8,512]{1,0:T(8,128)S(1)}, f32[8,512,512]{2,1,0:T(8,128)}) fusion(pred[512,512]{0,1:T(8,128)(4,1)S(1)} %compare_and_fusion.2, bf16[512,8,128]{0,2,1:T(8,128)(2,1)S(1)} %bitcast.88, bf16[512,8,128]{2,0,1:T(8,128)(2,1)} %get-tuple-element.307), kind=kOutput, calls=%fused_computation.10.clone.1 | convolution fusion | flops 543158272 | bytes 10764288 | tf_op jit(solution)/shard_map/while/body/eval_jaxpr/qhd,khd->hqk/dot_general | solution.py:102
  328.0 4.5 fusion.53
  333.1 8.5 %fusion.55 = f32[8,512,128]{2,1,0:T(8,128)} fusion(f32[8,512,128]{2,1,0:T(8,128)} %get-tuple-element.288, bf16[512,8,128]{0,2,1:T(8,128)(2,1)S(1)} %bitcast.92, f32[8,512,512]{2,1,0:T(8,128)} %get-tuple-element.268, f32[8,512]{1,0:T(8,128)S(1)} %select_maximum_fusion.2, pred[512,512]{0,1:T(8,128)(4,1)S(1)} %compare_and_fusion.2, ...), kind=kOutput, calls=%fused_computation.16.clone.1 | convolution fusion | flops 548929536 | bytes 13926401 | tf_op jit(solution)/shard_map/while/body/eval_jaxpr/hqk,khd->hqd/dot_general | solution.py:110
  341.6 3.1 gather_fusion
  347.3 6.1 %fusion.52 = (f32[8,512]{1,0:T(8,128)S(1)}, f32[8,512,512]{2,1,0:T(8,128)}) fusion(pred[512,512]{0,1:T(8,128)(4,1)S(1)} %compare_and_fusion.2, bf16[512,8,128]{0,2,1:T(8,128)(2,1)S(1)} %bitcast.88, bf16[512,8,128]{2,0,1:T(8,128)(2,1)} %get-tuple-element.307), kind=kOutput, calls=%fused_computation.10.clone.1 | convolution fusion | flops 543158272 | bytes 10764288 | tf_op jit(solution)/shard_map/while/body/eval_jaxpr/qhd,khd->hqk/dot_general | solution.py:102
  353.4 4.5 fusion.53
  358.5 8.5 %fusion.55 = f32[8,512,128]{2,1,0:T(8,128)} fusion(f32[8,512,128]{2,1,0:T(8,128)} %get-tuple-element.288, bf16[512,8,128]{0,2,1:T(8,128)(2,1)S(1)} %bitcast.92, f32[8,512,512]{2,1,0:T(8,128)} %get-tuple-element.268, f32[8,512]{1,0:T(8,128)S(1)} %select_maximum_fusion.2, pred[512,512]{0,1:T(8,128)(4,1)S(1)} %compare_and_fusion.2, ...), kind=kOutput, calls=%fused_computation.16.clone.1 | convolution fusion | flops 548929536 | bytes 13926401 | tf_op jit(solution)/shard_map/while/body/eval_jaxpr/hqk,khd->hqd/dot_general | solution.py:110
  366.9 3.1 gather_fusion
  372.7 6.1 %fusion.52 = (f32[8,512]{1,0:T(8,128)S(1)}, f32[8,512,512]{2,1,0:T(8,128)}) fusion(pred[512,512]{0,1:T(8,128)(4,1)S(1)} %compare_and_fusion.2, bf16[512,8,128]{0,2,1:T(8,128)(2,1)S(1)} %bitcast.88, bf16[512,8,128]{2,0,1:T(8,128)(2,1)} %get-tuple-element.307), kind=kOutput, calls=%fused_computation.10.clone.1 | convolution fusion | flops 543158272 | bytes 10764288 | tf_op jit(solution)/shard_map/while/body/eval_jaxpr/qhd,khd->hqk/dot_general | solution.py:102
  378.8 4.5 fusion.53
  383.8 8.5 %fusion.55 = f32[8,512,128]{2,1,0:T(8,128)} fusion(f32[8,512,128]{2,1,0:T(8,128)} %get-tuple-element.288, bf16[512,8,128]{0,2,1:T(8,128)(2,1)S(1)} %bitcast.92, f32[8,512,512]{2,1,0:T(8,128)} %get-tuple-element.268, f32[8,512]{1,0:T(8,128)S(1)} %select_maximum_fusion.2, pred[512,512]{0,1:T(8,128)(4,1)S(1)} %compare_and_fusion.2, ...), kind=kOutput, calls=%fused_computation.16.clone.1 | convolution fusion | flops 548929536 | bytes 13926401 | tf_op jit(solution)/shard_map/while/body/eval_jaxpr/hqk,khd->hqd/dot_general | solution.py:110
  392.3 3.1 gather_fusion
  398.1 6.1 %fusion.52 = (f32[8,512]{1,0:T(8,128)S(1)}, f32[8,512,512]{2,1,0:T(8,128)}) fusion(pred[512,512]{0,1:T(8,128)(4,1)S(1)} %compare_and_fusion.2, bf16[512,8,128]{0,2,1:T(8,128)(2,1)S(1)} %bitcast.88, bf16[512,8,128]{2,0,1:T(8,128)(2,1)} %get-tuple-element.307), kind=kOutput, calls=%fused_computation.10.clone.1 | convolution fusion | flops 543158272 | bytes 10764288 | tf_op jit(solution)/shard_map/while/body/eval_jaxpr/qhd,khd->hqk/dot_general | solution.py:102
  404.2 4.5 fusion.53
  409.2 8.5 %fusion.55 = f32[8,512,128]{2,1,0:T(8,128)} fusion(f32[8,512,128]{2,1,0:T(8,128)} %get-tuple-element.288, bf16[512,8,128]{0,2,1:T(8,128)(2,1)S(1)} %bitcast.92, f32[8,512,512]{2,1,0:T(8,128)} %get-tuple-element.268, f32[8,512]{1,0:T(8,128)S(1)} %select_maximum_fusion.2, pred[512,512]{0,1:T(8,128)(4,1)S(1)} %compare_and_fusion.2, ...), kind=kOutput, calls=%fused_computation.16.clone.1 | convolution fusion | flops 548929536 | bytes 13926401 | tf_op jit(solution)/shard_map/while/body/eval_jaxpr/hqk,khd->hqd/dot_general | solution.py:110
  417.7 3.1 gather_fusion
  423.4 6.1 %fusion.52 = (f32[8,512]{1,0:T(8,128)S(1)}, f32[8,512,512]{2,1,0:T(8,128)}) fusion(pred[512,512]{0,1:T(8,128)(4,1)S(1)} %compare_and_fusion.2, bf16[512,8,128]{0,2,1:T(8,128)(2,1)S(1)} %bitcast.88, bf16[512,8,128]{2,0,1:T(8,128)(2,1)} %get-tuple-element.307), kind=kOutput, calls=%fused_computation.10.clone.1 | convolution fusion | flops 543158272 | bytes 10764288 | tf_op jit(solution)/shard_map/while/body/eval_jaxpr/qhd,khd->hqk/dot_general | solution.py:102
  429.6 4.5 fusion.53
  434.6 8.5 %fusion.55 = f32[8,512,128]{2,1,0:T(8,128)} fusion(f32[8,512,128]{2,1,0:T(8,128)} %get-tuple-element.288, bf16[512,8,128]{0,2,1:T(8,128)(2,1)S(1)} %bitcast.92, f32[8,512,512]{2,1,0:T(8,128)} %get-tuple-element.268, f32[8,512]{1,0:T(8,128)S(1)} %select_maximum_fusion.2, pred[512,512]{0,1:T(8,128)(4,1)S(1)} %compare_and_fusion.2, ...), kind=kOutput, calls=%fused_computation.16.clone.1 | convolution fusion | flops 548929536 | bytes 13926401 | tf_op jit(solution)/shard_map/while/body/eval_jaxpr/hqk,khd->hqd/dot_general | solution.py:110
  443.1 3.1 gather_fusion
  448.8 6.1 %fusion.52 = (f32[8,512]{1,0:T(8,128)S(1)}, f32[8,512,512]{2,1,0:T(8,128)}) fusion(pred[512,512]{0,1:T(8,128)(4,1)S(1)} %compare_and_fusion.2, bf16[512,8,128]{0,2,1:T(8,128)(2,1)S(1)} %bitcast.88, bf16[512,8,128]{2,0,1:T(8,128)(2,1)} %get-tuple-element.307), kind=kOutput, calls=%fused_computation.10.clone.1 | convolution fusion | flops 543158272 | bytes 10764288 | tf_op jit(solution)/shard_map/while/body/eval_jaxpr/qhd,khd->hqk/dot_general | solution.py:102
  455.0 4.5 fusion.53
  460.0 8.5 %fusion.55 = f32[8,512,128]{2,1,0:T(8,128)} fusion(f32[8,512,128]{2,1,0:T(8,128)} %get-tuple-element.288, bf16[512,8,128]{0,2,1:T(8,128)(2,1)S(1)} %bitcast.92, f32[8,512,512]{2,1,0:T(8,128)} %get-tuple-element.268, f32[8,512]{1,0:T(8,128)S(1)} %select_maximum_fusion.2, pred[512,512]{0,1:T(8,128)(4,1)S(1)} %compare_and_fusion.2, ...), kind=kOutput, calls=%fused_computation.16.clone.1 | convolution fusion | flops 548929536 | bytes 13926401 | tf_op jit(solution)/shard_map/while/body/eval_jaxpr/hqk,khd->hqd/dot_general | solution.py:110
  470.7 9.5 %fusion.13 = bf16[4096,512]{0,1:T(8,128)(2,1)} fusion(bf16[512,1024]{0,1:T(8,128)(2,1)S(1)} %bitcast.98, bf16[1024,4096]{1,0:T(8,128)(2,1)} %param.19), kind=kOutput, calls=%fused_computation.31 | convolution fusion | flops 4297064448 | bytes 13631488 | tf_op jit(solution)/shard_map/dot_general | solution.py:166
  481.0 3.8 sort.107
  484.8 2.8 gather_fusion.4
  487.6 4.0 all-to-all-start.2
  491.5 2.8 gather_fusion.6
  494.3 23.4 %all-to-all-done.2 = bf16[8,64,1024]{2,1,0:T(8,128)(2,1)S(1)} async-done(((bf16[8,64,1024]{2,1,0:T(8,128)(2,1)}), bf16[8,64,1024]{2,1,0:T(8,128)(2,1)S(1)}, u32[]{:S(2)}, u32[]{:S(2)}) %all-to-all-start.2) | async-done | bytes 1048608 | tf_op jit(solution)/shard_map/all_to_all | solution.py:127
  517.8 3.6 all-to-all-start.3
  521.3 3.8 sort.104
  525.1 6.4 %reduce-scatter.2.cloned.1.call-done = bf16[1024,512]{0,1:T(8,128)(2,1)} async-done(((bf16[4096,512]{0,1:T(8,128)(2,1)}), bf16[1024,512]{0,1:T(8,128)(2,1)}) %reduce-scatter.2.cloned.1.call-update) | async-done | bytes 1048592 | tf_op jit(solution)/shard_map/reduce_scatter | solution.py:165
  533.0 8.9 %psum.23 = f32[512]{0:T(512)S(1)} all-reduce(f32[512]{0:T(512)S(1)} %fusion.14), channel_id=1, replica_groups=mesh['tok'=8,'rep'=4] {'rep'}, use_global_device_ids=true, to_apply=%region_12.13 | all-reduce | flops 512 | bytes 4096 | tf_op jit(solution)/shard_map/psum | solution.py:176
  542.0 2.0 fusion.18
  544.0 2.8 gather_fusion.2
  547.8 3.6 all-to-all-start.1
  551.4 5.8 sort.108
  558.0 3.8 sort.105
  561.7 3.8 sort.106
  565.5 3.8 sort.109
  569.3 3.8 sort.110
  573.1 2.8 gather_fusion.5
  575.9 2.8 gather_fusion.7
  578.6 2.8 gather_fusion.3
  (142 shorter events, 43.5 us)
Async XLA Ops:
  10.9 5.3 copy-start.8
  10.9 5.5 copy-start.3
  10.9 5.6 copy-start
  10.9 53.9 %all-to-all-start = ((bf16[4,512,1024]{1,2,0:T(8,128)(2,1)}), bf16[4,512,1024]{1,2,0:T(8,128)(2,1)}, u32[]{:S(2)}, u32[]{:S(2)}) async-start(bf16[4,512,1024]{1,2,0:T(8,128)(2,1)} %stack.2), calls=%async_computation | async-start | bytes 8388608 | tf_op jit(solution)/shard_map/all_to_all | solution.py:70
  16.3 166.9 %all-gather.3.cloned.1.call-start = ((), (), s32[]{:S(2)}) async-start(), calls=%async_computation.5 | async-start | bytes 9437184 | tf_op jit(solution)/shard_map/all_gather | solution.py:138
  75.4 17.5 %copy-start.5 = (f32[1024]{0:T(1024)S(1)}, f32[1024]{0:T(1024)}, u32[]{:S(2)}) copy-start(f32[1024]{0:T(1024)} %param.21) | copy-start | bytes 12292
  95.2 0.7 copy-start.6
  100.5 165.4 %all-gather.5.cloned.1.call-start = ((), (), s32[]{:S(2)}) async-start(), calls=%async_computation.6 | async-start | bytes 9437184 | tf_op jit(solution)/shard_map/all_gather | solution.py:139
  110.7 420.8 %reduce-scatter.2.cloned.1.call-start = ((), (), s32[]{:S(2)}) async-start(), calls=%async_computation.7 | async-start | bytes 5242880 | tf_op jit(solution)/shard_map/reduce_scatter | solution.py:165
  480.2 0.7 copy-start.4
  480.2 4.6 copy-start.1
  487.6 4.0 copy-start.2
  487.6 30.2 %all-to-all-start.2 = ((bf16[8,64,1024]{2,1,0:T(8,128)(2,1)}), bf16[8,64,1024]{2,1,0:T(8,128)(2,1)S(1)}, u32[]{:S(2)}, u32[]{:S(2)}) async-start(bf16[8,64,1024]{2,1,0:T(8,128)(2,1)} %bitcast.13), calls=%async_computation.3 | async-start | bytes 2097152 | tf_op jit(solution)/shard_map/all_to_all | solution.py:127
  494.3 47.6 %copy-start.7 = (f32[1024]{0:T(1024)S(1)}, f32[1024]{0:T(1024)}, u32[]{:S(2)}) copy-start(f32[1024]{0:T(1024)} %param.22) | copy-start | bytes 12292
  517.8 30.1 %all-to-all-start.3 = ((bf16[8,64,1024]{2,1,0:T(8,128)(2,1)}), bf16[8,64,1024]{2,1,0:T(8,128)(2,1)S(1)}, u32[]{:S(2)}, u32[]{:S(2)}) async-start(bf16[8,64,1024]{2,1,0:T(8,128)(2,1)} %bitcast.15), calls=%async_computation.4 | async-start | bytes 2097152 | tf_op jit(solution)/shard_map/all_to_all | solution.py:130
  547.8 30.8 %all-to-all-start.1 = ((bf16[8,64,1024]{2,1,0:T(8,128)(2,1)}), bf16[8,64,1024]{2,1,0:T(8,128)(2,1)S(1)}, u32[]{:S(2)}, u32[]{:S(2)}) async-start(bf16[8,64,1024]{2,1,0:T(8,128)(2,1)} %bitcast.95), calls=%async_computation.2 | async-start | bytes 2097152 | tf_op jit(solution)/shard_map/all_to_all | solution.py:182
Sparse Core Ops, SparseCore 0:
  100.6 82.5 all-gather.2
  185.4 80.5 all-gather.4
  480.4 51.1 reduce-scatter.1
